TPU v7x, 32 devices: a whole 2x2x4 slice. The times are simulated.
32 devices in a mesh: groups: 2 (over y), slab: 16 (over z, x, core).
Axes of the slice: x: 2, y: 2, z: 4, core: 2. Of those that a mesh axis runs over, the one named last changes fastest.
Arguments:
- rhs: float32 [2, 64, 128, 128], P('groups', 'slab'), parts along dimension 0, may hold values from -6 to 6
- labels: int32 [64, 256, 128], P('slab', 'groups'), parts along dimension 1, may hold values from 0 to 4, as said below
- sigma_table: float32 [5, 3], replicated, may hold values from 0.05 to 2
Outputs:
- correction: float32 [2, 64, 128, 128], P('groups', 'slab'), parts along dimension 0
There are 2 independent parts, one for each index of `groups`. A program takes and returns all parts, laid end to end along the dimension named above; an argument that names none is the same for every part. Nothing has to cross between parts.
Inputs may be any that keep to these rules, and one draw needn't show every extreme that they name: Label 0 marks exactly the voxels outside an ellipsoid centred on the grid with semi-axes 0.45 * 128, 0.45 * 128 and 0.55 * 64 cells; inside, labels 1 to 4 are drawn independently for each voxel.
All inputs are finite; a program needn't handle non-finite values.
Results may differ from a plain program's by a relative error of at most 0.0002.
Values sent between devices are 32-bit elements; how exact they have to be, the bound alone decides.
A program may use at most 64 MiB of HBM per device.

v0:
```python
import jax
import jax.numpy as jnp
from jax import lax
from jax.sharding import PartitionSpec as P

LABELS = 5
OMEGA = 0.8


def extended_2(shard, sides, width):
    for axis, dim in sides:
        size, length = (lax.axis_size(axis), shard.shape[dim])
        up = [(i, (i + 1) % size) for i in range(size - 1)]
        down = [(j, i) for i, j in up]
        last = lax.slice_in_dim(shard, length - width, length, axis=dim)
        first = lax.slice_in_dim(shard, 0, width, axis=dim)
        before = lax.ppermute(last, axis, up)
        after = lax.ppermute(first, axis, down)
        shard = jnp.concatenate([before, shard, after], axis=dim)
    return shard


def harmonic(lower_side, upper_side):
    return 2.0 * lower_side * upper_side / (lower_side + upper_side)


def conductivity(padded, sigma_table, column):
    running = jnp.zeros(padded.shape, jnp.float32)
    for tissue in range(LABELS):
        running = running + jnp.where(padded == tissue, sigma_table[tissue, column], 0.0)
    return running


def coefficients(labels_ext, sigma_table):
    padded = jnp.pad(labels_ext, ((0, 0), (1, 1), (1, 1)))
    active = (padded > 0).astype(jnp.float32)
    sigma_x = conductivity(padded, sigma_table, 0)
    sigma_y = conductivity(padded, sigma_table, 1)
    sigma_z = conductivity(padded, sigma_table, 2)
    inner_x = harmonic(sigma_x[1:-1, :-1, 1:-1], sigma_x[1:-1, 1:, 1:-1])
    couple_x = inner_x * active[1:-1, :-1, 1:-1] * active[1:-1, 1:, 1:-1]
    inner_y = harmonic(sigma_y[1:-1, 1:-1, :-1], sigma_y[1:-1, 1:-1, 1:])
    couple_y = inner_y * active[1:-1, 1:-1, :-1] * active[1:-1, 1:-1, 1:]
    inner_z = harmonic(sigma_z[:-1, 1:-1, 1:-1], sigma_z[1:, 1:-1, 1:-1])
    couple_z = inner_z * active[:-1, 1:-1, 1:-1] * active[1:, 1:-1, 1:-1]
    centre_mask = active[1:-1, 1:-1, 1:-1]
    faces = (
        inner_x[:, :-1]
        + inner_x[:, 1:]
        + inner_y[:, :, :-1]
        + inner_y[:, :, 1:]
        + inner_z[:-1]
        + inner_z[1:]
    )
    diagonal = centre_mask * faces + (1.0 - centre_mask)
    return (centre_mask, diagonal, couple_x, couple_y, couple_z)


def operate(extended, terms):
    couple_x, couple_y, couple_z = (terms[2], terms[3], terms[4])
    centre = extended[:, 1:-1]
    widened = jnp.pad(centre, ((0, 0), (0, 0), (1, 1), (1, 1)))
    neighbours = (
        couple_x[:, :-1] * widened[:, :, :-2, 1:-1] + couple_x[:, 1:] * widened[:, :, 2:, 1:-1]
    )
    neighbours = (
        neighbours
        + couple_y[:, :, :-1] * widened[:, :, 1:-1, :-2]
        + couple_y[:, :, 1:] * widened[:, :, 1:-1, 2:]
    )
    neighbours = neighbours + couple_z[:-1] * extended[:, :-2] + couple_z[1:] * extended[:, 2:]
    return terms[1] * centre - neighbours


def smooth(extended, source, terms):
    image = operate(extended, terms)
    return extended[:, 1:-1] + OMEGA * terms[0] * (source - image) / terms[1]


def start(source, terms):
    return OMEGA * terms[0] * source / terms[1]


def leftover(extended, source, terms):
    return terms[0] * (source - operate(extended, terms))


def pair_matrix(length):
    rows_index = lax.broadcasted_iota(jnp.int32, (length, length // 2), 0)
    cols_index = lax.broadcasted_iota(jnp.int32, (length, length // 2), 1)
    return (rows_index // 2 == cols_index).astype(jnp.float32)


def pair_sum(values, along):
    if along == values.ndim - 1:
        return jnp.matmul(values, pair_matrix(values.shape[-1]), precision=lax.Precision.HIGHEST)
    folded = values.shape[:along] + (values.shape[along] // 2, 2) + values.shape[along + 1 :]
    return jnp.sum(values.reshape(folded), axis=along + 1)


def coarsen(terms):
    centre_mask, diagonal, couple_x, couple_y, couple_z = terms
    coarse_x = pair_sum(pair_sum(couple_x[:, 0::2], 0), 2)
    coarse_y = pair_sum(pair_sum(couple_y[:, :, 0::2], 0), 1)
    coarse_z = pair_sum(pair_sum(couple_z[0::2], 1), 2)
    internal = (
        pair_sum(pair_sum(couple_x[:, 1::2], 0), 2)
        + pair_sum(pair_sum(couple_y[:, :, 1::2], 0), 1)
        + pair_sum(pair_sum(couple_z[1::2], 1), 2)
    )
    counted = pair_sum(pair_sum(pair_sum(centre_mask, 0), 1), 2)
    raw_diag = pair_sum(pair_sum(pair_sum(centre_mask * diagonal, 0), 1), 2) - 2.0 * internal
    coarse_mask = jnp.minimum(counted, 1.0)
    coarse_diag = raw_diag + (1.0 - coarse_mask)
    return ((coarse_mask, coarse_diag, coarse_x, coarse_y, coarse_z), raw_diag)


def restrict(field):
    return pair_sum(pair_sum(pair_sum(field, 1), 2), 3)


def widen(field):
    sides, planes, rows_count, cols_count = field.shape
    spread = pair_matrix(2 * cols_count).T
    along_y = jnp.matmul(field, spread, precision=lax.Precision.HIGHEST)
    grown = jnp.broadcast_to(
        along_y[:, :, None, :, None, :], (sides, planes, 2, rows_count, 2, 2 * cols_count)
    )
    return grown.reshape(sides, 2 * planes, 2 * rows_count, 2 * cols_count)


def plane_total(values):
    return jnp.sum(values, axis=(-2, -1))


def line_terms(coarse_terms, raw_diag):
    line_diag = plane_total(raw_diag) - 2.0 * (
        plane_total(coarse_terms[2]) + plane_total(coarse_terms[3])
    )
    return (line_diag, plane_total(coarse_terms[4]))


def fine_rim(field):
    return extended_2(field, (("slab", 1),), 1)


def coarse_rim(field):
    return extended_2(field, (("slab", 1),), 1)


def on_device(rhs, labels, sigma_table):
    labels_near = extended_2(labels, (("slab", 0),), 1)
    own_terms = coefficients(labels_near, sigma_table)
    source = own_terms[0] * rhs
    fine_first = start(source, own_terms)
    fine_second = smooth(fine_rim(fine_first), source, own_terms)
    fine_left = leftover(fine_rim(fine_second), source, own_terms)
    coarse_terms, raw_diag = coarsen(own_terms)
    coarse_source = restrict(fine_left)
    coarse_first = start(coarse_source, coarse_terms)
    coarse_second = smooth(coarse_rim(coarse_first), coarse_source, coarse_terms)
    coarse_left = leftover(coarse_rim(coarse_second), coarse_source, coarse_terms)
    line_diag, line_faces = line_terms(coarse_terms, raw_diag)
    planes = line_diag.shape[0]
    local_rows = plane_total(coarse_left).T
    band = jnp.stack([line_diag, line_faces[:-1]], axis=1)
    all_rows, all_band = (
        lax.all_gather(local_rows, "slab", axis=0, tiled=True),
        lax.all_gather(band, "slab", axis=0, tiled=True),
    )
    lower_band = -all_band[:, 1]
    upper_band = -jnp.concatenate([all_band[1:, 1], jnp.zeros((1,), jnp.float32)])
    line_solution = lax.linalg.tridiagonal_solve(lower_band, all_band[:, 0], upper_band, all_rows)
    own_line = lax.dynamic_slice_in_dim(line_solution, lax.axis_index("slab") * planes, planes, 0)
    coarse_fix = coarse_second + coarse_terms[0] * own_line.T[:, :, None, None]
    coarse_post = smooth(coarse_rim(coarse_fix), coarse_source, coarse_terms)
    coarse_final = smooth(coarse_rim(coarse_post), coarse_source, coarse_terms)
    fine_third = fine_second + own_terms[0] * widen(coarse_final)
    fine_fourth = smooth(fine_rim(fine_third), source, own_terms)
    return smooth(fine_rim(fine_fourth), source, own_terms)


def solution(mesh):
    placed = (P("groups", "slab", None, None), P("slab", "groups", None), P())
    return jax.shard_map(
        on_device,
        mesh=mesh,
        in_specs=placed,
        out_specs=P("groups", "slab", None, None),
        check_vma=False,
    )
```

profile of v0, /device:TPU:8, one launch (start us, length us, event | category | flops | bytes accessed | tf_op | source)
XLA Modules:
  0.0 265.4 jit_solution(3007158552615316442)
XLA Ops:
  0.0 0.9 fusion.160
  0.9 2.7 %collective-permute-start.1 = (s32[1,128,128]{2,1,0:T(8,128)S(1)}, s32[1,128,128]{2,1,0:T(8,128)S(1)}, u32[]{:S(2)}, u32[]{:S(2)}) collective-permute-start(s32[1,128,128]{2,1,0:T(8,128)S(1)} %get-tuple-element.28), channel_id=1, source_target_pairs={{1,0},{2,1},{3,2},{4,3},{5,4},{6,5},{7,6},{8,7},{9,8},{10,9},{11,1... | collective-permute-start | bytes 196616 | tf_op jit(solution)/shard_map/ppermute | solution.py:18
  3.7 1.9 collective-permute-start
  5.6 0.7 copy-done.14
  6.3 0.7 fusion.169
  7.0 0.7 copy-done.15
  7.7 0.6 dynamic-slice
  8.9 1.2 collective-permute-done
  10.5 11.2 %select_add_fusion.2 = (f32[6,130,130]{2,1,0:T(8,128)S(1)}, f32[6,130,130]{2,1,0:T(8,128)}, f32[6,130,130]{2,1,0:T(8,128)S(1)}) fusion(f32[]{:T(128)} %bitcast.6, f32[]{:T(128)} %bitcast.5, f32[]{:T(128)} %bitcast.4, f32[]{:T(128)} %bitcast.3, f32[]{:T(128)} %bitcast.2, s32[6,128,128]{2,1,0:T(8,128)S(1)} %pad_add_fusion, f32[]{:T(128)} %bitcast.16, ...), kind=kLoop, calls=%fused_computation.29 | loop fusion | flops 3244800 | bytes 1610076 | tf_op jit(solution)/shard_map/add | solution.py:30
  22.1 0.7 slice.1108
  22.8 1.7 slice_multiply_fusion.2
  24.5 0.7 slice.1110
  25.2 0.7 slice.1121
  26.2 0.9 bitcast_reduce_fusion.2
  27.3 0.6 fusion.159
  28.0 3.3 %collective-permute-start.3 = (f32[1,1,128,128]{3,2,1,0:T(8,128)}, f32[1,1,128,128]{3,2,1,0:T(8,128)}, u32[]{:S(2)}, u32[]{:S(2)}) collective-permute-start(f32[1,1,128,128]{3,2,1,0:T(8,128)} %get-tuple-element.26), channel_id=1, source_target_pairs={{1,0},{2,1},{3,2},{4,3},{5,4},{6,5},{7,6},{8,7},{9,8},{10,9},{11,1... | collective-permute-start | bytes 196616 | tf_op jit(solution)/shard_map/ppermute | solution.py:18
  31.3 1.9 collective-permute-start.2
  33.2 4.6 %slice.1109 = f32[4,128,64]{2,1,0:T(8,128)S(1)} slice(f32[4,128,129]{2,1,0:T(8,128)S(1)} %get-tuple-element.10), slice={[0:4:1], [0:128:1], [1:129:2]} | slice | bytes 262144 | tf_op jit(solution)/shard_map/slice | solution.py:108
  37.8 0.9 copy-done.6
  39.0 0.7 copy-done.7
  39.8 0.9 copy-done.8
  40.7 0.8 reduce_sum.187
  41.6 0.8 fusion.150
  43.0 0.7 fusion.165
  44.4 0.6 copy-done.10
  45.1 0.8 fusion.1
  45.9 4.5 %slice.1116 = f32[4,128,65]{2,1,0:T(8,128)S(1)} slice(f32[4,128,129]{2,1,0:T(8,128)S(1)} %get-tuple-element.10), slice={[0:4:1], [0:128:1], [0:129:2]} | slice | bytes 266240 | tf_op jit(solution)/shard_map/slice | solution.py:104
  50.5 0.7 copy.36
  51.3 0.7 copy.35
  52.2 1.2 fusion.13
  53.4 0.7 fusion.158
  54.1 4.5 %collective-permute-start.5 = (f32[1,1,128,128]{3,2,1,0:T(8,128)}, f32[1,1,128,128]{3,2,1,0:T(8,128)S(1)}, u32[]{:S(2)}, u32[]{:S(2)}) collective-permute-start(f32[1,1,128,128]{3,2,1,0:T(8,128)} %get-tuple-element.24), channel_id=1, source_target_pairs={{1,0},{2,1},{3,2},{4,3},{5,4},{6,5},{7,6},{8,7},{9,8},{10,9},{11,1... | collective-permute-start | bytes 196616 | tf_op jit(solution)/shard_map/ppermute | solution.py:18
  58.6 1.9 collective-permute-start.4
  60.9 4.4 %collective-permute-done.4 = f32[1,1,128,128]{3,2,1,0:T(8,128)S(1)} collective-permute-done((f32[1,1,128,128]{3,2,1,0:T(8,128)}, f32[1,1,128,128]{3,2,1,0:T(8,128)S(1)}, u32[]{:S(2)}, u32[]{:S(2)}) %collective-permute-start.4) | collective-permute-done | bytes 65568 | tf_op jit(solution)/shard_map/ppermute | solution.py:17
  66.0 0.6 copy-done
  66.9 15.3 %all-gather.1 = f32[16,2,2]{2,1,0:T(2,128)S(1)} all-gather(f32[1,2,2]{2,1,0:T(2,128)S(1)} %bitcast.570), channel_id=1, replica_groups=mesh['groups'=2,'slab'=16] {'slab'}, dimensions={0}, use_global_device_ids=true | all-gather | bytes 272 | tf_op jit(solution)/shard_map/all_gather | solution.py:169
  82.2 0.6 fusion.168
  83.0 0.7 fusion.167
  83.7 6.0 %collective-permute-start.7 = (f32[1,1,64,64]{3,2,1,0:T(8,128)S(1)}, f32[1,1,64,64]{3,2,1,0:T(8,128)S(1)}, u32[]{:S(2)}, u32[]{:S(2)}) collective-permute-start(f32[1,1,64,64]{3,2,1,0:T(8,128)S(1)} %get-tuple-element.40), channel_id=1, source_target_pairs={{1,0},{2,1},{3,2},{4,3},{5,4},{6,5},{7,6},{8,7},{9,8},{10,9},{11,1... | collective-permute-start | bytes 49160 | tf_op jit(solution)/shard_map/ppermute | solution.py:18
  89.7 1.9 collective-permute-start.6
  91.9 0.7 fusion.172
  92.6 0.7 fusion.170
  93.3 0.7 fusion.175
  94.0 1.8 collective-permute-done.6
  96.0 2.8 %collective-permute-start.9 = (f32[1,1,64,64]{3,2,1,0:T(8,128)S(1)}, f32[1,1,64,64]{3,2,1,0:T(8,128)S(1)}, u32[]{:S(2)}, u32[]{:S(2)}) collective-permute-start(f32[1,1,64,64]{3,2,1,0:T(8,128)S(1)} %get-tuple-element.36), channel_id=1, source_target_pairs={{1,0},{2,1},{3,2},{4,3},{5,4},{6,5},{7,6},{8,7},{9,8},{10,9},{11,1... | collective-permute-start | bytes 49160 | tf_op jit(solution)/shard_map/ppermute | solution.py:18
  98.7 2.1 collective-permute-start.8
  100.9 0.7 fusion.174
  160.8 24.9 %all-reduce.9 = f32[32]{0:T(128)S(1)} all-reduce(f32[32]{0:T(128)S(1)} %dynamic-update-slice), channel_id=2, replica_groups=mesh['groups'=2,'slab'=16] {'slab'}, use_global_device_ids=true, to_apply=%add.9 | all-reduce | flops 32 | bytes 256
  185.7 0.7 fusion.173
  186.4 0.7 fusion.171
  228.9 1.9 collective-permute-start.11
  230.8 2.4 collective-permute-start.10
  233.2 3.7 %collective-permute-done.10 = f32[1,1,64,64]{3,2,1,0:T(8,128)S(1)} collective-permute-done((f32[1,1,64,64]{3,2,1,0:T(8,128)S(1)}, f32[1,1,64,64]{3,2,1,0:T(8,128)S(1)}, u32[]{:S(2)}, u32[]{:S(2)}) %collective-permute-start.10) | collective-permute-done | bytes 16416 | tf_op jit(solution)/shard_map/ppermute | solution.py:17
  237.1 2.7 %collective-permute-start.13 = (f32[1,1,64,64]{3,2,1,0:T(8,128)S(1)}, f32[1,1,64,64]{3,2,1,0:T(8,128)S(1)}, u32[]{:S(2)}, u32[]{:S(2)}) collective-permute-start(f32[1,1,64,64]{3,2,1,0:T(8,128)S(1)} %get-tuple-element.30), channel_id=1, source_target_pairs={{1,0},{2,1},{3,2},{4,3},{5,4},{6,5},{7,6},{8,7},{9,8},{10,9},{11,1... | collective-permute-start | bytes 49160 | tf_op jit(solution)/shard_map/ppermute | solution.py:18
  239.8 1.9 collective-permute-start.12
  241.7 4.8 %collective-permute-done.12 = f32[1,1,64,64]{3,2,1,0:T(8,128)S(1)} collective-permute-done((f32[1,1,64,64]{3,2,1,0:T(8,128)S(1)}, f32[1,1,64,64]{3,2,1,0:T(8,128)S(1)}, u32[]{:S(2)}, u32[]{:S(2)}) %collective-permute-start.12) | collective-permute-done | bytes 16416 | tf_op jit(solution)/shard_map/ppermute | solution.py:17
  247.1 1.9 collective-permute-start.15
  249.0 2.4 collective-permute-start.14
  251.4 4.1 %collective-permute-done.14 = f32[1,1,128,128]{3,2,1,0:T(8,128)S(1)} collective-permute-done((f32[1,1,128,128]{3,2,1,0:T(8,128)S(1)}, f32[1,1,128,128]{3,2,1,0:T(8,128)S(1)}, u32[]{:S(2)}, u32[]{:S(2)}) %collective-permute-start.14) | collective-permute-done | bytes 65568 | tf_op jit(solution)/shard_map/ppermute | solution.py:17
  255.5 0.4 fusion.39
  255.9 1.9 collective-permute-start.17
  257.9 2.4 collective-permute-start.16
  260.3 4.1 %collective-permute-done.16 = f32[1,1,128,128]{3,2,1,0:T(8,128)S(1)} collective-permute-done((f32[1,1,128,128]{3,2,1,0:T(8,128)S(1)}, f32[1,1,128,128]{3,2,1,0:T(8,128)S(1)}, u32[]{:S(2)}, u32[]{:S(2)}) %collective-permute-start.16) | collective-permute-done | bytes 65568 | tf_op jit(solution)/shard_map/ppermute | solution.py:17
  264.4 1.1 fusion.53
  (92 shorter events, 6.6 us)
Async XLA Ops:
  0.0 10.1 %copy-start.4 = (s32[4,128,128]{2,1,0:T(8,128)S(1)}, s32[4,128,128]{2,1,0:T(8,128)}, u32[]{:S(2)}) copy-start(s32[4,128,128]{2,1,0:T(8,128)} %param.4) | copy-start | bytes 786436
  0.9 8.0 %collective-permute-start.1 = (s32[1,128,128]{2,1,0:T(8,128)S(1)}, s32[1,128,128]{2,1,0:T(8,128)S(1)}, u32[]{:S(2)}, u32[]{:S(2)}) collective-permute-start(s32[1,128,128]{2,1,0:T(8,128)S(1)} %get-tuple-element.28), channel_id=1, source_target_pairs={{1,0},{2,1},{3,2},{4,3},{5,4},{6,5},{7,6},{8,7},{9,8},{10,9},{11,1... | collective-permute-start | bytes 196616 | tf_op jit(solution)/shard_map/ppermute | solution.py:18
  3.7 6.5 %collective-permute-start = (s32[1,128,128]{2,1,0:T(8,128)S(1)}, s32[1,128,128]{2,1,0:T(8,128)S(1)}, u32[]{:S(2)}, u32[]{:S(2)}) collective-permute-start(s32[1,128,128]{2,1,0:T(8,128)S(1)} %get-tuple-element.27), channel_id=1, source_target_pairs={{0,1},{1,2},{2,3},{3,4},{4,5},{5,6},{6,7},{7,8},{8,9},{9,10},{10,1... | collective-permute-start | bytes 196616 | tf_op jit(solution)/shard_map/ppermute | solution.py:17
  5.6 0.7 copy-start.14
  7.0 0.7 copy-start.15
  26.2 1.0 copy-start.9
  28.0 24.2 %collective-permute-start.3 = (f32[1,1,128,128]{3,2,1,0:T(8,128)}, f32[1,1,128,128]{3,2,1,0:T(8,128)}, u32[]{:S(2)}, u32[]{:S(2)}) collective-permute-start(f32[1,1,128,128]{3,2,1,0:T(8,128)} %get-tuple-element.26), channel_id=1, source_target_pairs={{1,0},{2,1},{3,2},{4,3},{5,4},{6,5},{7,6},{8,7},{9,8},{10,9},{11,1... | collective-permute-start | bytes 196616 | tf_op jit(solution)/shard_map/ppermute | solution.py:18
  31.3 20.9 %collective-permute-start.2 = (f32[1,1,128,128]{3,2,1,0:T(8,128)}, f32[1,1,128,128]{3,2,1,0:T(8,128)}, u32[]{:S(2)}, u32[]{:S(2)}) collective-permute-start(f32[1,1,128,128]{3,2,1,0:T(8,128)} %get-tuple-element.25), channel_id=1, source_target_pairs={{0,1},{1,2},{2,3},{3,4},{4,5},{5,6},{6,7},{7,8},{8,9},{9,10},{10,1... | collective-permute-start | bytes 196616 | tf_op jit(solution)/shard_map/ppermute | solution.py:17
  37.8 0.9 copy-start.6
  38.8 0.9 copy-start.7
  39.8 0.9 copy-start.8
  39.8 1.7 copy-start.5
  42.6 1.1 copy-start.3
  44.2 0.8 copy-start.10
  44.2 0.9 copy-start.11
  45.9 4.6 %copy-start.13 = (f32[2,64,64]{1,2,0:T(8,128)S(1)}, f32[2,64,64]{1,2,0:T(8,128)}, u32[]{:S(2)}) copy-start(f32[2,64,64]{1,2,0:T(8,128)} %get-tuple-element.38) | copy-start | bytes 98308
  50.5 0.8 copy-start.12
  54.1 6.9 %collective-permute-start.5 = (f32[1,1,128,128]{3,2,1,0:T(8,128)}, f32[1,1,128,128]{3,2,1,0:T(8,128)S(1)}, u32[]{:S(2)}, u32[]{:S(2)}) collective-permute-start(f32[1,1,128,128]{3,2,1,0:T(8,128)} %get-tuple-element.24), channel_id=1, source_target_pairs={{1,0},{2,1},{3,2},{4,3},{5,4},{6,5},{7,6},{8,7},{9,8},{10,9},{11,1... | collective-permute-start | bytes 196616 | tf_op jit(solution)/shard_map/ppermute | solution.py:18
  58.6 6.7 %collective-permute-start.4 = (f32[1,1,128,128]{3,2,1,0:T(8,128)}, f32[1,1,128,128]{3,2,1,0:T(8,128)S(1)}, u32[]{:S(2)}, u32[]{:S(2)}) collective-permute-start(f32[1,1,128,128]{3,2,1,0:T(8,128)} %get-tuple-element.23), channel_id=1, source_target_pairs={{0,1},{1,2},{2,3},{3,4},{4,5},{5,6},{6,7},{7,8},{8,9},{9,10},{10,1... | collective-permute-start | bytes 196616 | tf_op jit(solution)/shard_map/ppermute | solution.py:17
  65.8 0.8 copy-start
  83.6 12.2 %copy-start.2 = (f32[2,64,64]{2,1,0:T(8,128)S(1)}, f32[2,64,64]{2,1,0:T(8,128)}, u32[]{:S(2)}) copy-start(f32[2,64,64]{2,1,0:T(8,128)} %copy.35) | copy-start | bytes 98308
  83.7 12.2 %copy-start.1 = (f32[2,64,64]{2,1,0:T(8,128)S(1)}, f32[2,64,64]{2,1,0:T(8,128)}, u32[]{:S(2)}) copy-start(f32[2,64,64]{2,1,0:T(8,128)} %copy.36) | copy-start | bytes 98308
  83.7 10.4 %collective-permute-start.7 = (f32[1,1,64,64]{3,2,1,0:T(8,128)S(1)}, f32[1,1,64,64]{3,2,1,0:T(8,128)S(1)}, u32[]{:S(2)}, u32[]{:S(2)}) collective-permute-start(f32[1,1,64,64]{3,2,1,0:T(8,128)S(1)} %get-tuple-element.40), channel_id=1, source_target_pairs={{1,0},{2,1},{3,2},{4,3},{5,4},{6,5},{7,6},{8,7},{9,8},{10,9},{11,1... | collective-permute-start | bytes 49160 | tf_op jit(solution)/shard_map/ppermute | solution.py:18
  89.7 6.1 %collective-permute-start.6 = (f32[1,1,64,64]{3,2,1,0:T(8,128)S(1)}, f32[1,1,64,64]{3,2,1,0:T(8,128)S(1)}, u32[]{:S(2)}, u32[]{:S(2)}) collective-permute-start(f32[1,1,64,64]{3,2,1,0:T(8,128)S(1)} %get-tuple-element.39), channel_id=1, source_target_pairs={{0,1},{1,2},{2,3},{3,4},{4,5},{5,6},{6,7},{7,8},{8,9},{9,10},{10,1... | collective-permute-start | bytes 49160 | tf_op jit(solution)/shard_map/ppermute | solution.py:17
  96.0 64.4 %collective-permute-start.9 = (f32[1,1,64,64]{3,2,1,0:T(8,128)S(1)}, f32[1,1,64,64]{3,2,1,0:T(8,128)S(1)}, u32[]{:S(2)}, u32[]{:S(2)}) collective-permute-start(f32[1,1,64,64]{3,2,1,0:T(8,128)S(1)} %get-tuple-element.36), channel_id=1, source_target_pairs={{1,0},{2,1},{3,2},{4,3},{5,4},{6,5},{7,6},{8,7},{9,8},{10,9},{11,1... | collective-permute-start | bytes 49160 | tf_op jit(solution)/shard_map/ppermute | solution.py:18
  98.7 61.6 %collective-permute-start.8 = (f32[1,1,64,64]{3,2,1,0:T(8,128)S(1)}, f32[1,1,64,64]{3,2,1,0:T(8,128)S(1)}, u32[]{:S(2)}, u32[]{:S(2)}) collective-permute-start(f32[1,1,64,64]{3,2,1,0:T(8,128)S(1)} %get-tuple-element.35), channel_id=1, source_target_pairs={{0,1},{1,2},{2,3},{3,4},{4,5},{5,6},{6,7},{7,8},{8,9},{9,10},{10,1... | collective-permute-start | bytes 49160 | tf_op jit(solution)/shard_map/ppermute | solution.py:17
  228.9 4.3 %collective-permute-start.11 = (f32[1,1,64,64]{3,2,1,0:T(8,128)S(1)}, f32[1,1,64,64]{3,2,1,0:T(8,128)S(1)}, u32[]{:S(2)}, u32[]{:S(2)}) collective-permute-start(f32[1,1,64,64]{3,2,1,0:T(8,128)S(1)} %get-tuple-element.32), channel_id=1, source_target_pairs={{1,0},{2,1},{3,2},{4,3},{5,4},{6,5},{7,6},{8,7},{9,8},{10,9},{11,1... | collective-permute-start | bytes 49160 | tf_op jit(solution)/shard_map/ppermute | solution.py:18
  230.8 6.1 %collective-permute-start.10 = (f32[1,1,64,64]{3,2,1,0:T(8,128)S(1)}, f32[1,1,64,64]{3,2,1,0:T(8,128)S(1)}, u32[]{:S(2)}, u32[]{:S(2)}) collective-permute-start(f32[1,1,64,64]{3,2,1,0:T(8,128)S(1)} %get-tuple-element.31), channel_id=1, source_target_pairs={{0,1},{1,2},{2,3},{3,4},{4,5},{5,6},{6,7},{7,8},{8,9},{9,10},{10,1... | collective-permute-start | bytes 49160 | tf_op jit(solution)/shard_map/ppermute | solution.py:17
  237.1 4.6 %collective-permute-start.13 = (f32[1,1,64,64]{3,2,1,0:T(8,128)S(1)}, f32[1,1,64,64]{3,2,1,0:T(8,128)S(1)}, u32[]{:S(2)}, u32[]{:S(2)}) collective-permute-start(f32[1,1,64,64]{3,2,1,0:T(8,128)S(1)} %get-tuple-element.30), channel_id=1, source_target_pairs={{1,0},{2,1},{3,2},{4,3},{5,4},{6,5},{7,6},{8,7},{9,8},{10,9},{11,1... | collective-permute-start | bytes 49160 | tf_op jit(solution)/shard_map/ppermute | solution.py:18
  239.8 6.8 %collective-permute-start.12 = (f32[1,1,64,64]{3,2,1,0:T(8,128)S(1)}, f32[1,1,64,64]{3,2,1,0:T(8,128)S(1)}, u32[]{:S(2)}, u32[]{:S(2)}) collective-permute-start(f32[1,1,64,64]{3,2,1,0:T(8,128)S(1)} %get-tuple-element.29), channel_id=1, source_target_pairs={{0,1},{1,2},{2,3},{3,4},{4,5},{5,6},{6,7},{7,8},{8,9},{9,10},{10,1... | collective-permute-start | bytes 49160 | tf_op jit(solution)/shard_map/ppermute | solution.py:17
  247.1 4.3 %collective-permute-start.15 = (f32[1,1,128,128]{3,2,1,0:T(8,128)S(1)}, f32[1,1,128,128]{3,2,1,0:T(8,128)S(1)}, u32[]{:S(2)}, u32[]{:S(2)}) collective-permute-start(f32[1,1,128,128]{3,2,1,0:T(8,128)S(1)} %get-tuple-element.22), channel_id=1, source_target_pairs={{1,0},{2,1},{3,2},{4,3},{5,4},{6,5},{7,6},{8,7},{9,8},{10,9},{11,1... | collective-permute-start | bytes 196616 | tf_op jit(solution)/shard_map/ppermute | solution.py:18
  249.0 6.5 %collective-permute-start.14 = (f32[1,1,128,128]{3,2,1,0:T(8,128)S(1)}, f32[1,1,128,128]{3,2,1,0:T(8,128)S(1)}, u32[]{:S(2)}, u32[]{:S(2)}) collective-permute-start(f32[1,1,128,128]{3,2,1,0:T(8,128)S(1)} %get-tuple-element.21), channel_id=1, source_target_pairs={{0,1},{1,2},{2,3},{3,4},{4,5},{5,6},{6,7},{7,8},{8,9},{9,10},{10,1... | collective-permute-start | bytes 196616 | tf_op jit(solution)/shard_map/ppermute | solution.py:17
  255.9 4.3 %collective-permute-start.17 = (f32[1,1,128,128]{3,2,1,0:T(8,128)S(1)}, f32[1,1,128,128]{3,2,1,0:T(8,128)S(1)}, u32[]{:S(2)}, u32[]{:S(2)}) collective-permute-start(f32[1,1,128,128]{3,2,1,0:T(8,128)S(1)} %get-tuple-element.20), channel_id=1, source_target_pairs={{1,0},{2,1},{3,2},{4,3},{5,4},{6,5},{7,6},{8,7},{9,8},{10,9},{11,1... | collective-permute-start | bytes 196616 | tf_op jit(solution)/shard_map/ppermute | solution.py:18
  257.9 6.5 %collective-permute-start.16 = (f32[1,1,128,128]{3,2,1,0:T(8,128)S(1)}, f32[1,1,128,128]{3,2,1,0:T(8,128)S(1)}, u32[]{:S(2)}, u32[]{:S(2)}) collective-permute-start(f32[1,1,128,128]{3,2,1,0:T(8,128)S(1)} %get-tuple-element.19), channel_id=1, source_target_pairs={{0,1},{1,2},{2,3},{3,4},{4,5},{5,6},{6,7},{7,8},{8,9},{9,10},{10,1... | collective-permute-start | bytes 196616 | tf_op jit(solution)/shard_map/ppermute | solution.py:17
where the time goes:
time: 268 us; the launch traced here: 265 us
  between operations  101 us (38%)
  starting transfers between devices  46.7 us (17%)
  blocking collectives  40.2 us (15%)
  local copies, waits for them, and re-layouts  28.7 us (11%)
  waiting for transfers between devices  24.1 us (9%)
  other arithmetic  21.2 us (8%)
  matrix products  3.07 us (1%)
    ppermute x9, starting transfers between devices, extended_2(): after = lax.ppermute(first, axis, down)  27.8 us
    unnamed x1, blocking collectives  24.9 us
    ppermute x9, waiting for transfers between devices, extended_2(): before = lax.ppermute(last, axis, up)  24.1 us
    ppermute x9, starting transfers between devices, extended_2(): before = lax.ppermute(last, axis, up)  18.9 us
    all_gather x1, blocking collectives, on_device(): lax.all_gather(band, 'slab', axis=0, tiled=True)  15.3 us
    add x1, other arithmetic, conductivity(): running + jnp.where(padded == tissue, sigma_table[tissue, column], 0.0)  11.2 us
    unnamed x39, local copies, waits for them, and re-layouts  7.66 us
    slice x8, local copies, waits for them, and re-layouts, on_device(): lax.linalg.tridiagonal_solve(lower_band, all_band[:, 0], upper_band, all_...  5.56 us
  transfers between devices with their start and end apart: 18, of which 7 were waited for; matrix products, arithmetic and copies ran while one was open for 8% of the time, Pallas kernels for 0%

commit v1 on v0

--- a/solution.py
+++ b/solution.py
@@ -5,6 +5,32 @@
 
 LABELS = 5
 OMEGA = 0.8
+
+
+def create_the_pipes(view):
+    axis_id = "slab"
+    tall = lax.axis_size(axis_id)
+    odd = lax.axis_index(axis_id)
+    e_now, local_part, block_now = (tall, odd, view.shape[0])
+    buffer = [(to_i, (to_i + 1) % e_now) for to_i in range(e_now)]
+    copies = [(to_i, (to_i - 1) % e_now) for to_i in range(e_now)]
+    parts_out = jnp.zeros((*view.shape[:0], e_now * block_now, *view.shape[1:]), view.dtype)
+    parts_out = lax.dynamic_update_slice_in_dim(parts_out, view, local_part * block_now, axis=0)
+    vec_out = long_array = view
+    u_next = e_now // 2
+    hop_no = 1
+    while hop_no < u_next + 1:
+        vec_out = lax.ppermute(vec_out, axis_id, buffer)
+        parts_out = lax.dynamic_update_slice_in_dim(
+            parts_out, vec_out, (local_part - hop_no) % e_now * block_now, axis=0
+        )
+        if hop_no < e_now - u_next:
+            long_array = lax.ppermute(long_array, axis_id, copies)
+            parts_out = lax.dynamic_update_slice_in_dim(
+                parts_out, long_array, (local_part + hop_no) % e_now * block_now, axis=0
+            )
+        hop_no = hop_no + 1
+    return parts_out
 
 
 def extended_2(shard, sides, width):
@@ -166,7 +192,7 @@
     band = jnp.stack([line_diag, line_faces[:-1]], axis=1)
     all_rows, all_band = (
         lax.all_gather(local_rows, "slab", axis=0, tiled=True),
-        lax.all_gather(band, "slab", axis=0, tiled=True),
+        create_the_pipes(band),
     )
     lower_band = -all_band[:, 1]
     upper_band = -jnp.concatenate([all_band[1:, 1], jnp.zeros((1,), jnp.float32)])

time: 268 us -> 287 us (1.071)
  starting transfers between devices: 46.7 us -> 66 us
  blocking collectives: 40.2 us -> 29.6 us
  waiting for transfers between devices: 24.1 us -> 30.6 us
  local copies, waits for them, and re-layouts: 28.7 us -> 31.6 us
    ppermute x0 -> x15, starting transfers between devices: none -> 18.4 us  [the longest x7 18.2 us: create_the_pipes(): long_array = lax.ppermute(long_array, axis_id, copies)]
    all_gather x1 -> x0, blocking collectives: 15.3 us -> none  [on_device(): lax.all_gather(band, 'slab', axis=0, tiled=True)]
    ppermute x0 -> x15, waiting for transfers between devices: none -> 8.79 us  [the longest x8 8.52 us: create_the_pipes(): vec_out = lax.ppermute(vec_out, axis_id, buffer)]
    unnamed x1, blocking collectives: 24.9 us -> 29.6 us
    dynamic_update_slice x0 -> x16, local copies, waits for them, and re-layouts: none -> 3.24 us  [the longest x7 1.61 us: create_the_pipes(): lax.dynamic_update_slice_in_dim(parts_out, long_array, (local_part + hop_...]
  transfers between devices with their start and end apart: 18 -> 33, of which waited for: 7 -> 18; matrix products, arithmetic and copies ran while one was open for 8% -> 9% of each run, Pallas kernels for 0% -> 0%
where the time goes in v1:
time: 287 us; the launch traced here: 285 us
  between operations  102 us (36%)
  starting transfers between devices  66 us (23%)
  local copies, waits for them, and re-layouts  31.6 us (11%)
  waiting for transfers between devices  30.6 us (11%)
  blocking collectives  29.6 us (10%)
  other arithmetic  21.9 us (8%)
  matrix products  3.07 us (1%)
    unnamed x1, blocking collectives  29.6 us
    ppermute x9, starting transfers between devices, extended_2(): after = lax.ppermute(first, axis, down)  28.5 us
    ppermute x9, waiting for transfers between devices, extended_2(): before = lax.ppermute(last, axis, up)  21.8 us
    ppermute x9, starting transfers between devices, extended_2(): before = lax.ppermute(last, axis, up)  19.2 us
    ppermute x7, starting transfers between devices, create_the_pipes(): long_array = lax.ppermute(long_array, axis_id, copies)  18.2 us
    add x1, other arithmetic, conductivity(): running + jnp.where(padded == tissue, sigma_table[tissue, column], 0.0)  11.2 us
    ppermute x8, waiting for transfers between devices, create_the_pipes(): vec_out = lax.ppermute(vec_out, axis_id, buffer)  8.52 us
    unnamed x39, local copies, waits for them, and re-layouts  7.43 us
  transfers between devices with their start and end apart: 33, of which 18 were waited for; matrix products, arithmetic and copies ran while one was open for 9% of the time, Pallas kernels for 0%

profile of v1, /device:TPU:8, one launch (start us, length us, event | category | flops | bytes accessed | tf_op | source)
XLA Modules:
  0.0 284.6 jit_solution(8431064376320469304)
XLA Ops:
  0.0 0.9 fusion.160
  0.9 2.9 %collective-permute-start.1 = (s32[1,128,128]{2,1,0:T(8,128)S(1)}, s32[1,128,128]{2,1,0:T(8,128)S(1)}, u32[]{:S(2)}, u32[]{:S(2)}) collective-permute-start(s32[1,128,128]{2,1,0:T(8,128)S(1)} %get-tuple-element.28), channel_id=1, source_target_pairs={{1,0},{2,1},{3,2},{4,3},{5,4},{6,5},{7,6},{8,7},{9,8},{10,9},{11,1... | collective-permute-start | bytes 196616 | tf_op jit(solution)/shard_map/ppermute | solution.py:44
  3.8 1.9 collective-permute-start
  6.6 0.7 fusion.167
  9.3 0.9 collective-permute-done
  10.6 11.2 %select_add_fusion.2 = (f32[6,130,130]{2,1,0:T(8,128)S(1)}, f32[6,130,130]{2,1,0:T(8,128)}, f32[6,130,130]{2,1,0:T(8,128)S(1)}) fusion(f32[]{:T(128)} %bitcast.6, f32[]{:T(128)} %bitcast.5, f32[]{:T(128)} %bitcast.4, f32[]{:T(128)} %bitcast.3, f32[]{:T(128)} %bitcast.2, s32[6,128,128]{2,1,0:T(8,128)S(1)} %pad_add_fusion, f32[]{:T(128)} %bitcast.16, ...), kind=kLoop, calls=%fused_computation.29 | loop fusion | flops 3244800 | bytes 1610076 | tf_op jit(solution)/shard_map/add | solution.py:56
  22.9 1.7 slice_multiply_fusion.2
  26.3 1.0 bitcast_reduce_fusion.2
  28.1 3.6 %collective-permute-start.3 = (f32[1,1,128,128]{3,2,1,0:T(8,128)}, f32[1,1,128,128]{3,2,1,0:T(8,128)}, u32[]{:S(2)}, u32[]{:S(2)}) collective-permute-start(f32[1,1,128,128]{3,2,1,0:T(8,128)} %get-tuple-element.26), channel_id=1, source_target_pairs={{1,0},{2,1},{3,2},{4,3},{5,4},{6,5},{7,6},{8,7},{9,8},{10,9},{11,1... | collective-permute-start | bytes 196616 | tf_op jit(solution)/shard_map/ppermute | solution.py:44
  31.7 1.9 collective-permute-start.2
  33.7 4.6 %slice.1109 = f32[4,128,64]{2,1,0:T(8,128)S(1)} slice(f32[4,128,129]{2,1,0:T(8,128)S(1)} %get-tuple-element.10), slice={[0:4:1], [0:128:1], [1:129:2]} | slice | bytes 262144 | tf_op jit(solution)/shard_map/slice | solution.py:134
  38.3 0.9 copy-done.6
  39.5 0.7 copy-done.7
  41.1 0.8 reduce_sum.187
  42.1 0.8 fusion.150
  43.5 0.7 fusion.165
  46.1 0.8 fusion.1
  46.9 4.5 %slice.1116 = f32[4,128,65]{2,1,0:T(8,128)S(1)} slice(f32[4,128,129]{2,1,0:T(8,128)S(1)} %get-tuple-element.10), slice={[0:4:1], [0:128:1], [0:129:2]} | slice | bytes 266240 | tf_op jit(solution)/shard_map/slice | solution.py:130
  51.5 0.7 copy.21
  52.4 0.7 copy.20
  53.2 1.2 fusion.13
  55.1 4.5 %collective-permute-start.5 = (f32[1,1,128,128]{3,2,1,0:T(8,128)}, f32[1,1,128,128]{3,2,1,0:T(8,128)S(1)}, u32[]{:S(2)}, u32[]{:S(2)}) collective-permute-start(f32[1,1,128,128]{3,2,1,0:T(8,128)} %get-tuple-element.24), channel_id=1, source_target_pairs={{1,0},{2,1},{3,2},{4,3},{5,4},{6,5},{7,6},{8,7},{9,8},{10,9},{11,1... | collective-permute-start | bytes 196616 | tf_op jit(solution)/shard_map/ppermute | solution.py:44
  59.6 1.9 collective-permute-start.4
  61.9 4.4 %collective-permute-done.4 = f32[1,1,128,128]{3,2,1,0:T(8,128)S(1)} collective-permute-done((f32[1,1,128,128]{3,2,1,0:T(8,128)}, f32[1,1,128,128]{3,2,1,0:T(8,128)S(1)}, u32[]{:S(2)}, u32[]{:S(2)}) %collective-permute-start.4) | collective-permute-done | bytes 65568 | tf_op jit(solution)/shard_map/ppermute | solution.py:43
  67.9 2.6 collective-permute-start.11
  70.5 1.9 collective-permute-start.7
  72.4 2.4 collective-permute-start.6
  75.2 2.6 collective-permute-start.13
  78.2 0.8 collective-permute-done.12
  79.1 2.6 collective-permute-start.15
  82.1 0.8 collective-permute-done.14
  83.0 2.6 collective-permute-start.17
  86.0 0.8 collective-permute-done.16
  86.9 2.6 collective-permute-start.19
  89.8 0.9 collective-permute-done.18
  90.8 2.6 collective-permute-start.21
  93.8 0.8 collective-permute-done.20
  94.7 2.6 collective-permute-start.23
  97.7 0.8 collective-permute-done.22
  99.0 3.4 %collective-permute-done.24 = f32[2,2]{0,1:T(2,128)S(1)} collective-permute-done((f32[2,2]{0,1:T(2,128)S(1)}, f32[2,2]{0,1:T(2,128)S(1)}, u32[]{:S(2)}, u32[]{:S(2)}) %collective-permute-start.24) | collective-permute-done | bytes 48 | tf_op jit(solution)/shard_map/ppermute | solution.py:23
  102.6 0.7 fusion.169
  103.4 0.7 fusion.168
  104.2 0.7 fusion.172
  104.9 0.7 fusion.170
  105.6 0.7 fusion.175
  106.5 1.9 collective-permute-start.9
  108.5 2.4 collective-permute-start.8
  110.9 0.7 fusion.174
  170.9 29.6 %all-reduce.9 = f32[32]{0:T(128)S(1)} all-reduce(f32[32]{0:T(128)S(1)} %dynamic-update-slice), channel_id=2, replica_groups=mesh['groups'=2,'slab'=16] {'slab'}, use_global_device_ids=true, to_apply=%add.9 | all-reduce | flops 32 | bytes 256
  200.5 0.7 fusion.173
  201.2 0.7 fusion.171
  243.5 6.3 %collective-permute-start.26 = (f32[1,1,64,64]{3,2,1,0:T(8,128)S(1)}, f32[1,1,64,64]{3,2,1,0:T(8,128)S(1)}, u32[]{:S(2)}, u32[]{:S(2)}) collective-permute-start(f32[1,1,64,64]{3,2,1,0:T(8,128)S(1)} %get-tuple-element.32), channel_id=1, source_target_pairs={{1,0},{2,1},{3,2},{4,3},{5,4},{6,5},{7,6},{8,7},{9,8},{10,9},{11,1... | collective-permute-start | bytes 49160 | tf_op jit(solution)/shard_map/ppermute | solution.py:44
  249.8 1.9 collective-permute-start.25
  251.8 4.2 %collective-permute-done.25 = f32[1,1,64,64]{3,2,1,0:T(8,128)S(1)} collective-permute-done((f32[1,1,64,64]{3,2,1,0:T(8,128)S(1)}, f32[1,1,64,64]{3,2,1,0:T(8,128)S(1)}, u32[]{:S(2)}, u32[]{:S(2)}) %collective-permute-start.25) | collective-permute-done | bytes 16416 | tf_op jit(solution)/shard_map/ppermute | solution.py:43
  256.1 3.5 %collective-permute-start.28 = (f32[1,1,64,64]{3,2,1,0:T(8,128)S(1)}, f32[1,1,64,64]{3,2,1,0:T(8,128)S(1)}, u32[]{:S(2)}, u32[]{:S(2)}) collective-permute-start(f32[1,1,64,64]{3,2,1,0:T(8,128)S(1)} %get-tuple-element.30), channel_id=1, source_target_pairs={{1,0},{2,1},{3,2},{4,3},{5,4},{6,5},{7,6},{8,7},{9,8},{10,9},{11,1... | collective-permute-start | bytes 49160 | tf_op jit(solution)/shard_map/ppermute | solution.py:44
  259.6 1.9 collective-permute-start.27
  261.5 4.2 %collective-permute-done.27 = f32[1,1,64,64]{3,2,1,0:T(8,128)S(1)} collective-permute-done((f32[1,1,64,64]{3,2,1,0:T(8,128)S(1)}, f32[1,1,64,64]{3,2,1,0:T(8,128)S(1)}, u32[]{:S(2)}, u32[]{:S(2)}) %collective-permute-start.27) | collective-permute-done | bytes 16416 | tf_op jit(solution)/shard_map/ppermute | solution.py:43
  266.2 1.9 collective-permute-start.30
  268.2 2.4 collective-permute-start.29
  270.6 4.1 %collective-permute-done.29 = f32[1,1,128,128]{3,2,1,0:T(8,128)S(1)} collective-permute-done((f32[1,1,128,128]{3,2,1,0:T(8,128)S(1)}, f32[1,1,128,128]{3,2,1,0:T(8,128)S(1)}, u32[]{:S(2)}, u32[]{:S(2)}) %collective-permute-start.29) | collective-permute-done | bytes 65568 | tf_op jit(solution)/shard_map/ppermute | solution.py:43
  275.1 1.9 collective-permute-start.32
  277.0 2.4 collective-permute-start.31
  279.4 4.1 %collective-permute-done.31 = f32[1,1,128,128]{3,2,1,0:T(8,128)S(1)} collective-permute-done((f32[1,1,128,128]{3,2,1,0:T(8,128)S(1)}, f32[1,1,128,128]{3,2,1,0:T(8,128)S(1)}, u32[]{:S(2)}, u32[]{:S(2)}) %collective-permute-start.31) | collective-permute-done | bytes 65568 | tf_op jit(solution)/shard_map/ppermute | solution.py:43
  283.5 1.1 fusion.53
  (136 shorter events, 18.3 us)
Async XLA Ops:
  0.9 9.4 %copy-start.4 = (s32[4,128,128]{2,1,0:T(8,128)S(1)}, s32[4,128,128]{2,1,0:T(8,128)}, u32[]{:S(2)}) copy-start(s32[4,128,128]{2,1,0:T(8,128)} %param.4) | copy-start | bytes 786436
  0.9 8.4 %collective-permute-start.1 = (s32[1,128,128]{2,1,0:T(8,128)S(1)}, s32[1,128,128]{2,1,0:T(8,128)S(1)}, u32[]{:S(2)}, u32[]{:S(2)}) collective-permute-start(s32[1,128,128]{2,1,0:T(8,128)S(1)} %get-tuple-element.28), channel_id=1, source_target_pairs={{1,0},{2,1},{3,2},{4,3},{5,4},{6,5},{7,6},{8,7},{9,8},{10,9},{11,1... | collective-permute-start | bytes 196616 | tf_op jit(solution)/shard_map/ppermute | solution.py:44
  3.8 6.5 %collective-permute-start = (s32[1,128,128]{2,1,0:T(8,128)S(1)}, s32[1,128,128]{2,1,0:T(8,128)S(1)}, u32[]{:S(2)}, u32[]{:S(2)}) collective-permute-start(s32[1,128,128]{2,1,0:T(8,128)S(1)} %get-tuple-element.27), channel_id=1, source_target_pairs={{0,1},{1,2},{2,3},{3,4},{4,5},{5,6},{6,7},{7,8},{8,9},{9,10},{10,1... | collective-permute-start | bytes 196616 | tf_op jit(solution)/shard_map/ppermute | solution.py:43
  5.9 0.7 copy-start.15
  7.3 0.7 copy-start.16
  26.3 1.0 copy-start.9
  28.1 25.1 %collective-permute-start.3 = (f32[1,1,128,128]{3,2,1,0:T(8,128)}, f32[1,1,128,128]{3,2,1,0:T(8,128)}, u32[]{:S(2)}, u32[]{:S(2)}) collective-permute-start(f32[1,1,128,128]{3,2,1,0:T(8,128)} %get-tuple-element.26), channel_id=1, source_target_pairs={{1,0},{2,1},{3,2},{4,3},{5,4},{6,5},{7,6},{8,7},{9,8},{10,9},{11,1... | collective-permute-start | bytes 196616 | tf_op jit(solution)/shard_map/ppermute | solution.py:44
  31.7 21.5 %collective-permute-start.2 = (f32[1,1,128,128]{3,2,1,0:T(8,128)}, f32[1,1,128,128]{3,2,1,0:T(8,128)}, u32[]{:S(2)}, u32[]{:S(2)}) collective-permute-start(f32[1,1,128,128]{3,2,1,0:T(8,128)} %get-tuple-element.25), channel_id=1, source_target_pairs={{0,1},{1,2},{2,3},{3,4},{4,5},{5,6},{6,7},{7,8},{8,9},{9,10},{10,1... | collective-permute-start | bytes 196616 | tf_op jit(solution)/shard_map/ppermute | solution.py:43
  38.2 0.9 copy-start.6
  39.3 0.9 copy-start.7
  40.2 0.9 copy-start.8
  40.8 1.1 copy-start.5
  43.1 1.1 copy-start.3
  44.4 0.8 copy-start.10
  45.3 0.8 copy-start.11
  45.3 0.9 copy-start.12
  46.9 4.6 %copy-start.14 = (f32[2,64,64]{1,2,0:T(8,128)S(1)}, f32[2,64,64]{1,2,0:T(8,128)}, u32[]{:S(2)}) copy-start(f32[2,64,64]{1,2,0:T(8,128)} %get-tuple-element.38) | copy-start | bytes 98308
  51.5 0.8 copy-start.13
  55.1 6.9 %collective-permute-start.5 = (f32[1,1,128,128]{3,2,1,0:T(8,128)}, f32[1,1,128,128]{3,2,1,0:T(8,128)S(1)}, u32[]{:S(2)}, u32[]{:S(2)}) collective-permute-start(f32[1,1,128,128]{3,2,1,0:T(8,128)} %get-tuple-element.24), channel_id=1, source_target_pairs={{1,0},{2,1},{3,2},{4,3},{5,4},{6,5},{7,6},{8,7},{9,8},{10,9},{11,1... | collective-permute-start | bytes 196616 | tf_op jit(solution)/shard_map/ppermute | solution.py:44
  59.6 6.7 %collective-permute-start.4 = (f32[1,1,128,128]{3,2,1,0:T(8,128)}, f32[1,1,128,128]{3,2,1,0:T(8,128)S(1)}, u32[]{:S(2)}, u32[]{:S(2)}) collective-permute-start(f32[1,1,128,128]{3,2,1,0:T(8,128)} %get-tuple-element.23), channel_id=1, source_target_pairs={{0,1},{1,2},{2,3},{3,4},{4,5},{5,6},{6,7},{7,8},{8,9},{9,10},{10,1... | collective-permute-start | bytes 196616 | tf_op jit(solution)/shard_map/ppermute | solution.py:43
  66.8 0.8 copy-start
  67.8 7.3 %collective-permute-start.10 = (f32[2,2]{0,1:T(2,128)S(1)}, f32[2,2]{0,1:T(2,128)S(1)}, u32[]{:S(2)}, u32[]{:S(2)}) collective-permute-start(f32[2,2]{0,1:T(2,128)S(1)} %pad_maximum_fusion.16), channel_id=1, source_target_pairs={{0,1},{1,2},{2,3},{3,4},{4,5},{5,6},{6,7},{7,8},{8,9},{9,10},{10,1... | collective-permute-start | bytes 56 | tf_op jit(solution)/shard_map/ppermute | solution.py:23
  67.9 7.3 %collective-permute-start.11 = (f32[2,2]{0,1:T(2,128)S(1)}, f32[2,2]{0,1:T(2,128)S(1)}, u32[]{:S(2)}, u32[]{:S(2)}) collective-permute-start(f32[2,2]{0,1:T(2,128)S(1)} %pad_maximum_fusion.16), channel_id=1, source_target_pairs={{0,15},{1,0},{2,1},{3,2},{4,3},{5,4},{6,5},{7,6},{8,7},{9,8},{10,9... | collective-permute-start | bytes 56 | tf_op jit(solution)/shard_map/ppermute | solution.py:28
  70.5 35.8 %collective-permute-start.7 = (f32[1,1,64,64]{3,2,1,0:T(8,128)S(1)}, f32[1,1,64,64]{3,2,1,0:T(8,128)S(1)}, u32[]{:S(2)}, u32[]{:S(2)}) collective-permute-start(f32[1,1,64,64]{3,2,1,0:T(8,128)S(1)} %get-tuple-element.40), channel_id=1, source_target_pairs={{1,0},{2,1},{3,2},{4,3},{5,4},{6,5},{7,6},{8,7},{9,8},{10,9},{11,1... | collective-permute-start | bytes 49160 | tf_op jit(solution)/shard_map/ppermute | solution.py:44
  72.4 33.9 %collective-permute-start.6 = (f32[1,1,64,64]{3,2,1,0:T(8,128)S(1)}, f32[1,1,64,64]{3,2,1,0:T(8,128)S(1)}, u32[]{:S(2)}, u32[]{:S(2)}) collective-permute-start(f32[1,1,64,64]{3,2,1,0:T(8,128)S(1)} %get-tuple-element.39), channel_id=1, source_target_pairs={{0,1},{1,2},{2,3},{3,4},{4,5},{5,6},{6,7},{7,8},{8,9},{9,10},{10,1... | collective-permute-start | bytes 49160 | tf_op jit(solution)/shard_map/ppermute | solution.py:43
  75.1 3.9 %collective-permute-start.12 = (f32[2,2]{0,1:T(2,128)S(1)}, f32[2,2]{0,1:T(2,128)S(1)}, u32[]{:S(2)}, u32[]{:S(2)}) collective-permute-start(f32[2,2]{0,1:T(2,128)S(1)} %collective-permute-done.10), channel_id=1, source_target_pairs={{0,1},{1,2},{2,3},{3,4},{4,5},{5,6},{6,7},{7,8},{8,9},{9,10},{10,1... | collective-permute-start | bytes 56 | tf_op jit(solution)/shard_map/ppermute | solution.py:23
  75.2 3.9 %collective-permute-start.13 = (f32[2,2]{0,1:T(2,128)S(1)}, f32[2,2]{0,1:T(2,128)S(1)}, u32[]{:S(2)}, u32[]{:S(2)}) collective-permute-start(f32[2,2]{0,1:T(2,128)S(1)} %collective-permute-done.11), channel_id=1, source_target_pairs={{0,15},{1,0},{2,1},{3,2},{4,3},{5,4},{6,5},{7,6},{8,7},{9,8},{10,9... | collective-permute-start | bytes 56 | tf_op jit(solution)/shard_map/ppermute | solution.py:28
  78.2 28.1 %copy-start.1 = (f32[2,64,64]{2,1,0:T(8,128)S(1)}, f32[2,64,64]{2,1,0:T(8,128)}, u32[]{:S(2)}) copy-start(f32[2,64,64]{2,1,0:T(8,128)} %copy.21) | copy-start | bytes 98308
  78.2 28.1 %copy-start.2 = (f32[2,64,64]{2,1,0:T(8,128)S(1)}, f32[2,64,64]{2,1,0:T(8,128)}, u32[]{:S(2)}) copy-start(f32[2,64,64]{2,1,0:T(8,128)} %copy.20) | copy-start | bytes 98308
  79.1 3.9 %collective-permute-start.14 = (f32[2,2]{0,1:T(2,128)S(1)}, f32[2,2]{0,1:T(2,128)S(1)}, u32[]{:S(2)}, u32[]{:S(2)}) collective-permute-start(f32[2,2]{0,1:T(2,128)S(1)} %collective-permute-done.12), channel_id=1, source_target_pairs={{0,1},{1,2},{2,3},{3,4},{4,5},{5,6},{6,7},{7,8},{8,9},{9,10},{10,1... | collective-permute-start | bytes 56 | tf_op jit(solution)/shard_map/ppermute | solution.py:23
  79.1 3.9 %collective-permute-start.15 = (f32[2,2]{0,1:T(2,128)S(1)}, f32[2,2]{0,1:T(2,128)S(1)}, u32[]{:S(2)}, u32[]{:S(2)}) collective-permute-start(f32[2,2]{0,1:T(2,128)S(1)} %collective-permute-done.13), channel_id=1, source_target_pairs={{0,15},{1,0},{2,1},{3,2},{4,3},{5,4},{6,5},{7,6},{8,7},{9,8},{10,9... | collective-permute-start | bytes 56 | tf_op jit(solution)/shard_map/ppermute | solution.py:28
  83.0 3.9 %collective-permute-start.16 = (f32[2,2]{0,1:T(2,128)S(1)}, f32[2,2]{0,1:T(2,128)S(1)}, u32[]{:S(2)}, u32[]{:S(2)}) collective-permute-start(f32[2,2]{0,1:T(2,128)S(1)} %collective-permute-done.14), channel_id=1, source_target_pairs={{0,1},{1,2},{2,3},{3,4},{4,5},{5,6},{6,7},{7,8},{8,9},{9,10},{10,1... | collective-permute-start | bytes 56 | tf_op jit(solution)/shard_map/ppermute | solution.py:23
  83.0 3.9 %collective-permute-start.17 = (f32[2,2]{0,1:T(2,128)S(1)}, f32[2,2]{0,1:T(2,128)S(1)}, u32[]{:S(2)}, u32[]{:S(2)}) collective-permute-start(f32[2,2]{0,1:T(2,128)S(1)} %collective-permute-done.15), channel_id=1, source_target_pairs={{0,15},{1,0},{2,1},{3,2},{4,3},{5,4},{6,5},{7,6},{8,7},{9,8},{10,9... | collective-permute-start | bytes 56 | tf_op jit(solution)/shard_map/ppermute | solution.py:28
  86.8 3.9 %collective-permute-start.18 = (f32[2,2]{0,1:T(2,128)S(1)}, f32[2,2]{0,1:T(2,128)S(1)}, u32[]{:S(2)}, u32[]{:S(2)}) collective-permute-start(f32[2,2]{0,1:T(2,128)S(1)} %collective-permute-done.16), channel_id=1, source_target_pairs={{0,1},{1,2},{2,3},{3,4},{4,5},{5,6},{6,7},{7,8},{8,9},{9,10},{10,1... | collective-permute-start | bytes 56 | tf_op jit(solution)/shard_map/ppermute | solution.py:23
  86.9 3.9 %collective-permute-start.19 = (f32[2,2]{0,1:T(2,128)S(1)}, f32[2,2]{0,1:T(2,128)S(1)}, u32[]{:S(2)}, u32[]{:S(2)}) collective-permute-start(f32[2,2]{0,1:T(2,128)S(1)} %collective-permute-done.17), channel_id=1, source_target_pairs={{0,15},{1,0},{2,1},{3,2},{4,3},{5,4},{6,5},{7,6},{8,7},{9,8},{10,9... | collective-permute-start | bytes 56 | tf_op jit(solution)/shard_map/ppermute | solution.py:28
  90.7 3.9 %collective-permute-start.20 = (f32[2,2]{0,1:T(2,128)S(1)}, f32[2,2]{0,1:T(2,128)S(1)}, u32[]{:S(2)}, u32[]{:S(2)}) collective-permute-start(f32[2,2]{0,1:T(2,128)S(1)} %collective-permute-done.18), channel_id=1, source_target_pairs={{0,1},{1,2},{2,3},{3,4},{4,5},{5,6},{6,7},{7,8},{8,9},{9,10},{10,1... | collective-permute-start | bytes 56 | tf_op jit(solution)/shard_map/ppermute | solution.py:23
  90.8 3.9 %collective-permute-start.21 = (f32[2,2]{0,1:T(2,128)S(1)}, f32[2,2]{0,1:T(2,128)S(1)}, u32[]{:S(2)}, u32[]{:S(2)}) collective-permute-start(f32[2,2]{0,1:T(2,128)S(1)} %collective-permute-done.19), channel_id=1, source_target_pairs={{0,15},{1,0},{2,1},{3,2},{4,3},{5,4},{6,5},{7,6},{8,7},{9,8},{10,9... | collective-permute-start | bytes 56 | tf_op jit(solution)/shard_map/ppermute | solution.py:28
  94.6 3.9 %collective-permute-start.22 = (f32[2,2]{0,1:T(2,128)S(1)}, f32[2,2]{0,1:T(2,128)S(1)}, u32[]{:S(2)}, u32[]{:S(2)}) collective-permute-start(f32[2,2]{0,1:T(2,128)S(1)} %collective-permute-done.20), channel_id=1, source_target_pairs={{0,1},{1,2},{2,3},{3,4},{4,5},{5,6},{6,7},{7,8},{8,9},{9,10},{10,1... | collective-permute-start | bytes 56 | tf_op jit(solution)/shard_map/ppermute | solution.py:23
  94.7 4.0 %collective-permute-start.23 = (f32[2,2]{0,1:T(2,128)S(1)}, f32[2,2]{0,1:T(2,128)S(1)}, u32[]{:S(2)}, u32[]{:S(2)}) collective-permute-start(f32[2,2]{0,1:T(2,128)S(1)} %collective-permute-done.21), channel_id=1, source_target_pairs={{0,15},{1,0},{2,1},{3,2},{4,3},{5,4},{6,5},{7,6},{8,7},{9,8},{10,9... | collective-permute-start | bytes 56 | tf_op jit(solution)/shard_map/ppermute | solution.py:28
  98.5 3.9 %collective-permute-start.24 = (f32[2,2]{0,1:T(2,128)S(1)}, f32[2,2]{0,1:T(2,128)S(1)}, u32[]{:S(2)}, u32[]{:S(2)}) collective-permute-start(f32[2,2]{0,1:T(2,128)S(1)} %collective-permute-done.22), channel_id=1, source_target_pairs={{0,1},{1,2},{2,3},{3,4},{4,5},{5,6},{6,7},{7,8},{8,9},{9,10},{10,1... | collective-permute-start | bytes 56 | tf_op jit(solution)/shard_map/ppermute | solution.py:23
  106.5 63.9 %collective-permute-start.9 = (f32[1,1,64,64]{3,2,1,0:T(8,128)S(1)}, f32[1,1,64,64]{3,2,1,0:T(8,128)S(1)}, u32[]{:S(2)}, u32[]{:S(2)}) collective-permute-start(f32[1,1,64,64]{3,2,1,0:T(8,128)S(1)} %get-tuple-element.36), channel_id=1, source_target_pairs={{1,0},{2,1},{3,2},{4,3},{5,4},{6,5},{7,6},{8,7},{9,8},{10,9},{11,1... | collective-permute-start | bytes 49160 | tf_op jit(solution)/shard_map/ppermute | solution.py:44
  108.5 62.0 %collective-permute-start.8 = (f32[1,1,64,64]{3,2,1,0:T(8,128)S(1)}, f32[1,1,64,64]{3,2,1,0:T(8,128)S(1)}, u32[]{:S(2)}, u32[]{:S(2)}) collective-permute-start(f32[1,1,64,64]{3,2,1,0:T(8,128)S(1)} %get-tuple-element.35), channel_id=1, source_target_pairs={{0,1},{1,2},{2,3},{3,4},{4,5},{5,6},{6,7},{7,8},{8,9},{9,10},{10,1... | collective-permute-start | bytes 49160 | tf_op jit(solution)/shard_map/ppermute | solution.py:43
  243.5 8.3 %collective-permute-start.26 = (f32[1,1,64,64]{3,2,1,0:T(8,128)S(1)}, f32[1,1,64,64]{3,2,1,0:T(8,128)S(1)}, u32[]{:S(2)}, u32[]{:S(2)}) collective-permute-start(f32[1,1,64,64]{3,2,1,0:T(8,128)S(1)} %get-tuple-element.32), channel_id=1, source_target_pairs={{1,0},{2,1},{3,2},{4,3},{5,4},{6,5},{7,6},{8,7},{9,8},{10,9},{11,1... | collective-permute-start | bytes 49160 | tf_op jit(solution)/shard_map/ppermute | solution.py:44
  249.8 6.1 %collective-permute-start.25 = (f32[1,1,64,64]{3,2,1,0:T(8,128)S(1)}, f32[1,1,64,64]{3,2,1,0:T(8,128)S(1)}, u32[]{:S(2)}, u32[]{:S(2)}) collective-permute-start(f32[1,1,64,64]{3,2,1,0:T(8,128)S(1)} %get-tuple-element.31), channel_id=1, source_target_pairs={{0,1},{1,2},{2,3},{3,4},{4,5},{5,6},{6,7},{7,8},{8,9},{9,10},{10,1... | collective-permute-start | bytes 49160 | tf_op jit(solution)/shard_map/ppermute | solution.py:43
  256.1 5.4 %collective-permute-start.28 = (f32[1,1,64,64]{3,2,1,0:T(8,128)S(1)}, f32[1,1,64,64]{3,2,1,0:T(8,128)S(1)}, u32[]{:S(2)}, u32[]{:S(2)}) collective-permute-start(f32[1,1,64,64]{3,2,1,0:T(8,128)S(1)} %get-tuple-element.30), channel_id=1, source_target_pairs={{1,0},{2,1},{3,2},{4,3},{5,4},{6,5},{7,6},{8,7},{9,8},{10,9},{11,1... | collective-permute-start | bytes 49160 | tf_op jit(solution)/shard_map/ppermute | solution.py:44
  259.6 6.1 %collective-permute-start.27 = (f32[1,1,64,64]{3,2,1,0:T(8,128)S(1)}, f32[1,1,64,64]{3,2,1,0:T(8,128)S(1)}, u32[]{:S(2)}, u32[]{:S(2)}) collective-permute-start(f32[1,1,64,64]{3,2,1,0:T(8,128)S(1)} %get-tuple-element.29), channel_id=1, source_target_pairs={{0,1},{1,2},{2,3},{3,4},{4,5},{5,6},{6,7},{7,8},{8,9},{9,10},{10,1... | collective-permute-start | bytes 49160 | tf_op jit(solution)/shard_map/ppermute | solution.py:43
  266.2 4.3 %collective-permute-start.30 = (f32[1,1,128,128]{3,2,1,0:T(8,128)S(1)}, f32[1,1,128,128]{3,2,1,0:T(8,128)S(1)}, u32[]{:S(2)}, u32[]{:S(2)}) collective-permute-start(f32[1,1,128,128]{3,2,1,0:T(8,128)S(1)} %get-tuple-element.22), channel_id=1, source_target_pairs={{1,0},{2,1},{3,2},{4,3},{5,4},{6,5},{7,6},{8,7},{9,8},{10,9},{11,1... | collective-permute-start | bytes 196616 | tf_op jit(solution)/shard_map/ppermute | solution.py:44
  268.2 6.5 %collective-permute-start.29 = (f32[1,1,128,128]{3,2,1,0:T(8,128)S(1)}, f32[1,1,128,128]{3,2,1,0:T(8,128)S(1)}, u32[]{:S(2)}, u32[]{:S(2)}) collective-permute-start(f32[1,1,128,128]{3,2,1,0:T(8,128)S(1)} %get-tuple-element.21), channel_id=1, source_target_pairs={{0,1},{1,2},{2,3},{3,4},{4,5},{5,6},{6,7},{7,8},{8,9},{9,10},{10,1... | collective-permute-start | bytes 196616 | tf_op jit(solution)/shard_map/ppermute | solution.py:43
  275.1 4.3 %collective-permute-start.32 = (f32[1,1,128,128]{3,2,1,0:T(8,128)S(1)}, f32[1,1,128,128]{3,2,1,0:T(8,128)S(1)}, u32[]{:S(2)}, u32[]{:S(2)}) collective-permute-start(f32[1,1,128,128]{3,2,1,0:T(8,128)S(1)} %get-tuple-element.20), channel_id=1, source_target_pairs={{1,0},{2,1},{3,2},{4,3},{5,4},{6,5},{7,6},{8,7},{9,8},{10,9},{11,1... | collective-permute-start | bytes 196616 | tf_op jit(solution)/shard_map/ppermute | solution.py:44
  277.0 6.5 %collective-permute-start.31 = (f32[1,1,128,128]{3,2,1,0:T(8,128)S(1)}, f32[1,1,128,128]{3,2,1,0:T(8,128)S(1)}, u32[]{:S(2)}, u32[]{:S(2)}) collective-permute-start(f32[1,1,128,128]{3,2,1,0:T(8,128)S(1)} %get-tuple-element.19), channel_id=1, source_target_pairs={{0,1},{1,2},{2,3},{3,4},{4,5},{5,6},{6,7},{7,8},{8,9},{9,10},{10,1... | collective-permute-start | bytes 196616 | tf_op jit(solution)/shard_map/ppermute | solution.py:43
